TPU v7x, 512 devices: a whole 4x4x16 slice. The times are simulated.
512 devices in a mesh: vec: 64 (over y, z), row: 8 (over x, core).
Axes of the slice: x: 4, y: 4, z: 16, core: 2. Of those that a mesh axis runs over, the one named last changes fastest.
Arguments:
- vectors: bfloat16 [8, 4096, 1024], P('row', 'vec'), may hold values from -6 to 6
- rotation: bfloat16 [1024, 1024], P(None, 'vec'), may hold values from -0.1875 to 0.1875
- blocks: bfloat16 [256, 8, 128, 128], P('row'), may hold values from -0.125 to 0.125
- column_blocks: int32 [256, 8], P('row'), may hold values from -2 to 257, as said below
Outputs:
- filtered: bfloat16 [8, 4096, 1024], P('row', 'vec')
Inputs may be any that keep to these rules, and one draw needn't show every extreme that they name: `column_blocks`: block row r of partition p = r // 32 lists 8 distinct column blocks between p * 32 - 2 and p * 32 + 33; the first block row of every partition lists the lowest of these and the last one the highest; column blocks outside 0 to 255 stand for zeros.
All inputs are finite; a program needn't handle non-finite values.
Results may differ from a plain program's by a relative error of at most 0.006.
Values may be sent and summed in bfloat16 or wider, within the bound.
A program may use at most 64 MiB of HBM per device.

v0:
```python
import jax
import jax.numpy as jnp
from jax import lax
from jax.sharding import PartitionSpec as P

BS = 128
HB = 2
STEPS = 4


centre = 0.3
half_width = 1.2


def with_halo(block, sides, width):
    for axis, dim in sides:
        count = lax.axis_size(axis)
        forward = [(i, i + 1) for i in range(count - 1)]
        backward = [(target, source) for source, target in forward]
        low = lax.ppermute(
            lax.slice_in_dim(block, block.shape[dim] - width, None, axis=dim), axis, forward
        )
        high = lax.ppermute(lax.slice_in_dim(block, 0, width, axis=dim), axis, backward)
        block = jnp.concatenate([low, block, high], axis=dim)
    return block


def apply_matrix(operand, blocks, offsets):
    extended = with_halo(operand, (("row", 1),), HB * BS)
    stacked = extended.reshape(extended.shape[0], -1, BS)
    picked = stacked[:, offsets]
    product = jnp.einsum("rjab,krjb->kra", blocks, picked, preferred_element_type=jnp.float32)
    return product.reshape(extended.shape[0], -1)


def filter_panel(vec_panel, blocks, offsets):
    previous = vec_panel.astype(jnp.float32)
    current = (apply_matrix(vec_panel, blocks, offsets) - centre * previous) / half_width
    for turn_index in range(STEPS - 1):
        operand = current.astype(jnp.bfloat16)
        following = (
            2.0 * (apply_matrix(operand, blocks, offsets) - centre * current) / half_width
            - previous
        )
        previous = current
        current = following
    return current.astype(jnp.bfloat16)


def local(vectors, rotation, blocks, column_blocks):
    local_rows = vectors[0]
    offsets = column_blocks - (lax.axis_index("row") * column_blocks.shape[0] - HB)
    contract = (((0,), (1,)), ((), ()))
    vec_panel = lax.dot_general(
        rotation,
        lax.all_gather(local_rows, "vec", axis=0, tiled=True),
        contract,
        preferred_element_type=jnp.float32,
    ).astype(jnp.bfloat16)
    filtered = filter_panel(vec_panel, blocks, offsets)
    returned = lax.all_to_all(filtered, "vec", split_axis=1, concat_axis=0, tiled=True)
    return jnp.transpose(returned)[None]


def solution(mesh):
    placed = (P("row", "vec", None), P(None, "vec"), P("row", None, None, None), P("row", None))
    return jax.shard_map(
        local, mesh=mesh, in_specs=placed, out_specs=P("row", "vec", None), check_vma=False
    )
```

profile of v0, /device:TPU:1, one launch (start us, length us, event | category | flops | bytes accessed | tf_op | source)
XLA Modules:
  0.0 266.6 jit_solution(13129486595092253713)
XLA Ops:
  8.1 156.6 %all-gather.3.cloned.1.call-done = bf16[1,4096,1024]{2,1,0:T(8,128)(2,1)} async-done(((bf16[1,64,1024]{2,1,0:T(8,128)(2,1)}), bf16[1,4096,1024]{2,1,0:T(8,128)(2,1)}) %all-gather.3.cloned.1.call-update) | async-done | bytes 8388624 | tf_op jit(solution)/shard_map/all_gather | solution.py:56
  164.7 5.7 %fusion.2 = bf16[16,4096]{1,0:T(8,128)(2,1)S(1)} fusion(bf16[1024,16]{0,1:T(8,128)(2,1)S(1)} %copy-done, bf16[1,4096,1024]{2,1,0:T(8,128)(2,1)} %all-gather.3.cloned.1.call-done), kind=kOutput, calls=%fused_computation.6 | convolution fusion | flops 134283264 | bytes 8552448 | tf_op jit(solution)/shard_map/dot_general | solution.py:54
  170.4 11.5 %collective-permute-start = (bf16[16,256]{1,0:T(8,128)(2,1)S(1)}, bf16[16,256]{1,0:T(8,128)(2,1)S(1)}, u32[]{:S(2)}, u32[]{:S(2)}) collective-permute-start(bf16[16,256]{1,0:T(8,128)(2,1)S(1)} %get-tuple-element.11), channel_id=1, source_target_pairs={{0,1},{1,2},{2,3},{3,4},{4,5},{5,6},{6,7},{8,9},{9,10},{10,11},{11... | collective-permute-start | bytes 24584 | tf_op jit(solution)/shard_map/ppermute | solution.py:20
  181.8 1.9 collective-permute-start.1
  183.8 3.0 %collective-permute-done.1 = bf16[16,256]{1,0:T(8,128)(2,1)S(1)} collective-permute-done((bf16[16,256]{1,0:T(8,128)(2,1)S(1)}, bf16[16,256]{1,0:T(8,128)(2,1)S(1)}, u32[]{:S(2)}, u32[]{:S(2)}) %collective-permute-start.1) | collective-permute-done | bytes 8224 | tf_op jit(solution)/shard_map/ppermute | solution.py:23
  186.8 0.9 gather_fusion
  187.7 5.7 %convolution_bitcast_fusion.3 = f32[32,2,8,128]{3,2,1,0:T(8,128)S(1)} fusion(bf16[16,32,8,128]{3,0,2,1:T(8,128)(2,1)S(1)} %bitcast.130, bf16[32,8,128,128]{3,2,1,0:T(8,128)(2,1)} %param.6), kind=kOutput, calls=%fused_computation.10 | convolution fusion | flops 134217728 | bytes 9699328 | tf_op jit(solution)/shard_map/rjab,krjb->kra/dot_general | solution.py:32
  193.4 1.9 collective-permute-start.2
  195.4 2.4 collective-permute-start.3
  197.8 2.6 collective-permute-done.3
  200.4 0.9 gather_fusion.1
  201.2 5.7 %convolution_bitcast_fusion.2 = f32[32,2,8,128]{3,2,1,0:T(8,128)S(1)} fusion(bf16[16,32,8,128]{3,0,2,1:T(8,128)(2,1)S(1)} %bitcast.131, bf16[32,8,128,128]{3,2,1,0:T(8,128)(2,1)} %param.6), kind=kOutput, calls=%fused_computation.9 | convolution fusion | flops 134217728 | bytes 9699328 | tf_op jit(solution)/shard_map/rjab,krjb->kra/dot_general | solution.py:32
  207.0 1.9 collective-permute-start.4
  209.0 2.4 collective-permute-start.5
  211.4 2.6 collective-permute-done.5
  214.0 0.9 gather_fusion.2
  214.8 5.7 %convolution_bitcast_fusion.1 = f32[32,2,8,128]{3,2,1,0:T(8,128)S(1)} fusion(bf16[16,32,8,128]{3,0,2,1:T(8,128)(2,1)S(1)} %bitcast.132, bf16[32,8,128,128]{3,2,1,0:T(8,128)(2,1)} %param.6), kind=kOutput, calls=%fused_computation.8 | convolution fusion | flops 134217728 | bytes 9699328 | tf_op jit(solution)/shard_map/rjab,krjb->kra/dot_general | solution.py:32
  220.6 1.9 collective-permute-start.6
  222.6 2.4 collective-permute-start.7
  225.0 2.6 collective-permute-done.7
  227.6 0.9 gather_fusion.3
  228.4 5.7 %convolution_bitcast_fusion = f32[32,2,8,128]{3,2,1,0:T(8,128)S(1)} fusion(bf16[16,32,8,128]{3,0,2,1:T(8,128)(2,1)S(1)} %bitcast.129, bf16[32,8,128,128]{3,2,1,0:T(8,128)(2,1)} %param.6), kind=kOutput, calls=%fused_computation.7 | convolution fusion | flops 134217728 | bytes 9699328 | tf_op jit(solution)/shard_map/rjab,krjb->kra/dot_general | solution.py:32
  234.9 23.9 %all_to_all.19 = bf16[64,2,512]{2,1,0:T(2,128)(2,1)S(1)} all-to-all(bf16[64,2,512]{2,1,0:T(2,128)(2,1)S(1)} %reshape.80), channel_id=1, replica_groups=mesh['vec'=64,'row'=8] {'vec'}, dimensions={0} | all-to-all | bytes 262144 | tf_op jit(solution)/shard_map/all_to_all | solution.py:61
  259.0 0.8 copy.24
  (28 shorter events, 3.0 us)
Async XLA Ops:
  6.5 158.2 %copy-start = (bf16[1024,16]{0,1:T(8,128)(2,1)S(1)}, bf16[1024,16]{0,1:T(8,128)(2,1)}, u32[]{:S(2)}) copy-start(bf16[1024,16]{0,1:T(8,128)(2,1)} %param.5) | copy-start | bytes 98308
  6.5 158.2 %all-gather.3.cloned.1.call-start = ((), (), s32[]{:S(2)}) async-start(), calls=%async_computation.1 | async-start | bytes 8519680 | tf_op jit(solution)/shard_map/all_gather | solution.py:56
  170.4 13.4 %collective-permute-start = (bf16[16,256]{1,0:T(8,128)(2,1)S(1)}, bf16[16,256]{1,0:T(8,128)(2,1)S(1)}, u32[]{:S(2)}, u32[]{:S(2)}) collective-permute-start(bf16[16,256]{1,0:T(8,128)(2,1)S(1)} %get-tuple-element.11), channel_id=1, source_target_pairs={{0,1},{1,2},{2,3},{3,4},{4,5},{5,6},{6,7},{8,9},{9,10},{10,11},{11... | collective-permute-start | bytes 24584 | tf_op jit(solution)/shard_map/ppermute | solution.py:20
  181.8 5.0 %collective-permute-start.1 = (bf16[16,256]{1,0:T(8,128)(2,1)S(1)}, bf16[16,256]{1,0:T(8,128)(2,1)S(1)}, u32[]{:S(2)}, u32[]{:S(2)}) collective-permute-start(bf16[16,256]{1,0:T(8,128)(2,1)S(1)} %get-tuple-element.12), channel_id=1, source_target_pairs={{1,0},{2,1},{3,2},{4,3},{5,4},{6,5},{7,6},{9,8},{10,9},{11,10},{12... | collective-permute-start | bytes 24584 | tf_op jit(solution)/shard_map/ppermute | solution.py:23
  193.4 4.3 %collective-permute-start.2 = (bf16[16,256]{1,0:T(8,128)(2,1)S(1)}, bf16[16,256]{1,0:T(8,128)(2,1)S(1)}, u32[]{:S(2)}, u32[]{:S(2)}) collective-permute-start(bf16[16,256]{1,0:T(8,128)(2,1)S(1)} %get-tuple-element.9), channel_id=1, source_target_pairs={{0,1},{1,2},{2,3},{3,4},{4,5},{5,6},{6,7},{8,9},{9,10},{10,11},{11... | collective-permute-start | bytes 24584 | tf_op jit(solution)/shard_map/ppermute | solution.py:20
  195.4 5.0 %collective-permute-start.3 = (bf16[16,256]{1,0:T(8,128)(2,1)S(1)}, bf16[16,256]{1,0:T(8,128)(2,1)S(1)}, u32[]{:S(2)}, u32[]{:S(2)}) collective-permute-start(bf16[16,256]{1,0:T(8,128)(2,1)S(1)} %get-tuple-element.10), channel_id=1, source_target_pairs={{1,0},{2,1},{3,2},{4,3},{5,4},{6,5},{7,6},{9,8},{10,9},{11,10},{12... | collective-permute-start | bytes 24584 | tf_op jit(solution)/shard_map/ppermute | solution.py:23
  207.0 4.3 %collective-permute-start.4 = (bf16[16,256]{1,0:T(8,128)(2,1)S(1)}, bf16[16,256]{1,0:T(8,128)(2,1)S(1)}, u32[]{:S(2)}, u32[]{:S(2)}) collective-permute-start(bf16[16,256]{1,0:T(8,128)(2,1)S(1)} %get-tuple-element.7), channel_id=1, source_target_pairs={{0,1},{1,2},{2,3},{3,4},{4,5},{5,6},{6,7},{8,9},{9,10},{10,11},{11... | collective-permute-start | bytes 24584 | tf_op jit(solution)/shard_map/ppermute | solution.py:20
  209.0 5.0 %collective-permute-start.5 = (bf16[16,256]{1,0:T(8,128)(2,1)S(1)}, bf16[16,256]{1,0:T(8,128)(2,1)S(1)}, u32[]{:S(2)}, u32[]{:S(2)}) collective-permute-start(bf16[16,256]{1,0:T(8,128)(2,1)S(1)} %get-tuple-element.8), channel_id=1, source_target_pairs={{1,0},{2,1},{3,2},{4,3},{5,4},{6,5},{7,6},{9,8},{10,9},{11,10},{12... | collective-permute-start | bytes 24584 | tf_op jit(solution)/shard_map/ppermute | solution.py:23
  220.6 4.3 %collective-permute-start.6 = (bf16[16,256]{1,0:T(8,128)(2,1)S(1)}, bf16[16,256]{1,0:T(8,128)(2,1)S(1)}, u32[]{:S(2)}, u32[]{:S(2)}) collective-permute-start(bf16[16,256]{1,0:T(8,128)(2,1)S(1)} %get-tuple-element.5), channel_id=1, source_target_pairs={{0,1},{1,2},{2,3},{3,4},{4,5},{5,6},{6,7},{8,9},{9,10},{10,11},{11... | collective-permute-start | bytes 24584 | tf_op jit(solution)/shard_map/ppermute | solution.py:20
  222.6 5.0 %collective-permute-start.7 = (bf16[16,256]{1,0:T(8,128)(2,1)S(1)}, bf16[16,256]{1,0:T(8,128)(2,1)S(1)}, u32[]{:S(2)}, u32[]{:S(2)}) collective-permute-start(bf16[16,256]{1,0:T(8,128)(2,1)S(1)} %get-tuple-element.6), channel_id=1, source_target_pairs={{1,0},{2,1},{3,2},{4,3},{5,4},{6,5},{7,6},{9,8},{10,9},{11,10},{12... | collective-permute-start | bytes 24584 | tf_op jit(solution)/shard_map/ppermute | solution.py:23
Sparse Core Ops, SparseCore 0:
  10.3 154.3 all-gather.2
where the time goes:
time: 267 us
  waiting for transfers between devices  168 us (63%)
  matrix products  28.3 us (11%)
  starting transfers between devices  26.3 us (10%)
  blocking collectives  23.9 us (9%)
  between operations  13.6 us (5%)
  local copies, waits for them, and re-layouts  5.21 us (2%)
    all_gather x1, waiting for transfers between devices, local(): lax.all_gather(local_rows, 'vec', axis=0, tiled=True)  157 us
    all_to_all x1, blocking collectives, local(): lax.all_to_all(filtered, 'vec', split_axis=1, concat_axis=0, tiled=True)  23.9 us
    dot_general x4, matrix products, apply_matrix(): jnp.einsum('rjab,krjb->kra', blocks, picked, preferred_element_type=jnp.f...  22.6 us
    ppermute x4, starting transfers between devices, with_halo(): lax.ppermute(lax.slice_in_dim(block, block.shape[dim] - width, None, axis...  17.3 us
    ppermute x4, waiting for transfers between devices, with_halo(): lax.ppermute(lax.slice_in_dim(block, 0, width, axis=dim), axis, backward)  10.7 us
    ppermute x4, starting transfers between devices, with_halo(): lax.ppermute(lax.slice_in_dim(block, 0, width, axis=dim), axis, backward)  9.07 us
    dot_general x1, matrix products, local(): lax.dot_general(rotation, lax.all_gather(local_rows, 'vec', axis=0, tiled...  5.65 us
  transfers between devices with their start and end apart: 9, of which 5 were waited for; matrix products, arithmetic and copies ran while one was open for 0% of the time, Pallas kernels for 0%

commit v1 on v0

v1 whole, which is shorter than its diff:
```python
import functools

import jax
import jax.numpy as jnp
from jax import lax
from jax.experimental import pallas as pl
from jax.experimental.pallas import tpu as pltpu
from jax.sharding import PartitionSpec as P

MESH = pl.DeviceIdType.MESH
BS = 128
HB = 2
NNZB = 8
RB = 32
Z = 16
CORES = 2
F32 = jnp.float32
BF16 = jnp.bfloat16

centre = 0.3
half_width = 1.2


def take_all(ref, sem):
    pltpu.make_async_copy(ref, ref, sem).wait()


def halves(first, second):
    low = lax.broadcasted_iota(jnp.int32, first.shape, first.ndim - 1) < 64
    axis = first.ndim - 1
    return (
        jnp.where(low, first, pltpu.roll(second, 64, axis)),
        jnp.where(low, pltpu.roll(first, 64, axis), second),
    )


def kernel(
    nvec, nrow,
    v_hbm, rt_hbm, blk_hbm, col, out_ref,
    v_in, rt_in, blk, send1, recv1, u0, u1, u2, u3, fa, fb, send2, recv2, rall, fbuf,
    in_sem, s1, r1, s2, r2, hs, hr, gs, gr,
):
    me = lax.axis_index("vec")
    row = lax.axis_index("row")
    core = lax.rem(row, CORES)
    yy = me // Z
    xs = nrow // CORES
    ys = nvec // Z
    first = row * RB - HB

    v_copy = pltpu.make_async_copy(v_hbm, v_in, in_sem.at[0])
    r_copy = pltpu.make_async_copy(rt_hbm, rt_in, in_sem.at[1])
    b_copies = [
        pltpu.make_async_copy(blk_hbm.at[pl.ds(8 * q, 8)], blk.at[pl.ds(8 * q, 8)], in_sem.at[2 + q])
        for q in range(4)
    ]
    v_copy.start()
    r_copy.start()
    for c in b_copies:
        c.start()

    barrier = pltpu.get_barrier_semaphore()

    def greet(k, _):
        pl.semaphore_signal(barrier, inc=1, device_id={"vec": lax.rem(me + k, nvec)}, device_id_type=MESH)
        return 0

    lax.fori_loop(1, nvec, greet, 0)
    for k in range(1, nrow):
        pl.semaphore_signal(barrier, inc=1, device_id={"row": lax.rem(row + k, nrow)}, device_id_type=MESH)

    v_copy.wait()
    r_copy.wait()
    for t in range(4):
        pair = jnp.concatenate(
            [v_in[:, 256 * t : 256 * t + 128], v_in[:, 256 * t + 128 : 256 * t + 256]], axis=0
        )
        turned = pair.astype(F32).T.reshape(16, 8, 128).astype(BF16)
        send1[pl.ds(16 * t, 16)] = turned
    recv1[me] = send1[me]
    rall[row, me] = rt_in[:, pl.ds(pl.multiple_of(row * 128, 128), 128)]
    zero = jnp.zeros((HB, 16, 128), BF16)
    for u in (u0, u1, u2, u3):

        @pl.when(row == 0)
        def _():
            u[pl.ds(0, HB)] = zero

        @pl.when(row == nrow - 1)
        def _():
            u[pl.ds(RB + HB, HB)] = zero

    pl.semaphore_wait(barrier, nvec - 1 + nrow - 1)

    def deal(k, _):
        d = lax.rem(me + k, nvec)
        pltpu.make_async_remote_copy(
            send1.at[d], recv1.at[me], s1, r1, device_id={"vec": d}, device_id_type=MESH
        ).start()
        return 0

    lax.fori_loop(1, nvec, deal, 0)

    def along_z(k, _):
        d = yy * Z + lax.rem(me + k, Z)
        pltpu.make_async_remote_copy(
            rall.at[row, me], rall.at[row, me], gs.at[0], gr.at[0],
            device_id={"vec": d}, device_id_type=MESH,
        ).start()
        return 0

    lax.fori_loop(1, Z, along_z, 0)

    def halo(step, u):
        up = pltpu.make_async_remote_copy(
            u.at[pl.ds(RB, HB)], u.at[pl.ds(0, HB)], hs.at[step, 0], hr.at[step, 0],
            device_id={"row": jnp.minimum(row + 1, nrow - 1)}, device_id_type=MESH,
        )
        down = pltpu.make_async_remote_copy(
            u.at[pl.ds(HB, HB)], u.at[pl.ds(RB + HB, HB)], hs.at[step, 1], hr.at[step, 1],
            device_id={"row": jnp.maximum(row - 1, 0)}, device_id_type=MESH,
        )
        return up, down

    def halo_start(step, u):
        up, down = halo(step, u)
        pl.when(row < nrow - 1)(up.start)
        pl.when(row > 0)(down.start)

    def halo_wait(step, u):
        up, down = halo(step, u)
        pl.when(row > 0)(up.wait_recv)
        pl.when(row < nrow - 1)(down.wait_recv)

    def halo_sent(step, u):
        up, down = halo(step, u)
        pl.when(row < nrow - 1)(up.wait_send)
        pl.when(row > 0)(down.wait_send)

    take_all(recv1.at[pl.ds(0, nvec - 1)], r1)
    parts = recv1[...].astype(F32).reshape(RB, 2, 8, 128)
    low, high = halves(parts[:, 0], parts[:, 1])
    start = jnp.concatenate([low, high], axis=1)
    u0[pl.ds(HB, RB)] = start.astype(BF16)
    fa[...] = start
    halo_start(0, u0)

    take_all(rall.at[0, pl.ds(0, Z - 1)], gr.at[0])
    for k in range(1, ys):
        d = lax.rem(me + k * Z, nvec)
        pltpu.make_async_remote_copy(
            rall.at[row, pl.ds(yy * Z, Z)], rall.at[row, pl.ds(yy * Z, Z)], gs.at[1], gr.at[1],
            device_id={"vec": d}, device_id_type=MESH,
        ).start()

    for c in b_copies:
        c.wait()

    def product(u, r):
        left = jnp.concatenate([u[jnp.clip(col[j, r] - first, 0, RB + 2 * HB - 1)] for j in range(NNZB)], axis=1)
        right = jnp.concatenate([blk[r, j] for j in range(NNZB)], axis=1)
        return lax.dot_general(left, right, (((1,), (1,)), ((), ())), preferred_element_type=F32)

    def rows_of(turn, u, current, other, following, r):
        if turn == 0:
            made = (product(u, r) - centre * current[r]) / half_width
        else:
            made = 2.0 * (product(u, r) - centre * current[r]) / half_width - other[r]
        other[r] = made
        if following is not None:
            following[r + HB] = made.astype(BF16)
        return made

    def turn_of(turn, u, current, other, following):
        edge = functools.partial(rows_of, turn, u, current, other, following)
        for r in (0, 1, RB - 2, RB - 1):
            edge(r)
        halo_start(turn + 1, following)

        def inner(r, _):
            edge(r)
            return 0

        lax.fori_loop(HB, RB - HB, inner, 0, unroll=2)

    halo_wait(0, u0)
    turn_of(0, u0, fa, fb, u1)
    take_all(rall.at[0, pl.ds(0, nvec - Z)], gr.at[1])
    for k in range(1, xs):
        pltpu.make_async_remote_copy(
            rall.at[row], rall.at[row], gs.at[2], gr.at[2],
            device_id={"row": lax.rem(row + k * CORES, nrow)}, device_id_type=MESH,
        ).start()
    mate = row + 1 - 2 * core
    pltpu.make_async_remote_copy(
        rall.at[row], rall.at[row], gs.at[3], gr.at[3], device_id={"row": mate}, device_id_type=MESH
    ).start()
    halo_wait(1, u1)
    turn_of(1, u1, fb, fa, u2)
    halo_wait(2, u2)
    turn_of(2, u2, fa, fb, u3)
    halo_wait(3, u3)

    def last(k, _):
        r = lax.rem(me // 2 + k, RB)
        made = rows_of(3, u3, fb, fa, None, r)
        even, odd = halves(made[:8], made[8:])
        send2[2 * r] = even.astype(BF16)
        send2[2 * r + 1] = odd.astype(BF16)
        for side in range(2):
            d = 2 * r + side

            @pl.when(d != me)
            def _():
                pltpu.make_async_remote_copy(
                    send2.at[d], recv2.at[me], s2, r2, device_id={"vec": d}, device_id_type=MESH
                ).start()

        return 0

    lax.fori_loop(0, RB, last, 0)
    recv2[me] = send2[me]

    take_all(rall.at[pl.ds(0, xs - 1)], gr.at[2])
    for k in range(1, xs):
        other = lax.rem(row + k * CORES, nrow)
        pltpu.make_async_remote_copy(
            rall.at[other], rall.at[other], gs.at[4], gr.at[4], device_id={"row": mate}, device_id_type=MESH
        ).start()

    take_all(recv2.at[pl.ds(0, nvec - 1)], r2)
    for t in range(4):
        turned = recv2[pl.ds(16 * t, 16)].astype(F32).reshape(128, 128).T.astype(BF16)
        fbuf[:, 256 * t : 256 * t + 128] = turned[:64]
        fbuf[:, 256 * t + 128 : 256 * t + 256] = turned[64:]

    take_all(rall.at[0], gr.at[3])
    take_all(rall.at[pl.ds(0, xs - 1)], gr.at[4])
    total = jnp.zeros((64, 1024), F32)
    for t in range(4):
        right = jnp.concatenate(
            [rall[2 * t].reshape(1024, 128), rall[2 * t + 1].reshape(1024, 128)], axis=1
        )
        total += lax.dot_general(
            fbuf[:, 256 * t : 256 * t + 256], right, (((1,), (1,)), ((), ())), preferred_element_type=F32
        )
    out_ref[...] = total.astype(BF16)

    take_all(send1.at[pl.ds(0, nvec - 1)], s1)
    take_all(send2.at[pl.ds(0, nvec - 1)], s2)
    for step, u in enumerate((u0, u1, u2, u3)):
        halo_sent(step, u)
    take_all(rall.at[0, pl.ds(0, Z - 1)], gs.at[0])
    take_all(rall.at[0, pl.ds(0, nvec - Z)], gs.at[1])
    take_all(rall.at[pl.ds(0, xs - 1)], gs.at[2])
    take_all(rall.at[0], gs.at[3])
    take_all(rall.at[pl.ds(0, xs - 1)], gs.at[4])


def local(nvec, nrow, vectors, rotation, blocks, column_blocks):
    whole = pl.BlockSpec(memory_space=pltpu.HBM)
    out = pl.pallas_call(
        functools.partial(kernel, nvec, nrow),
        out_shape=jax.ShapeDtypeStruct((64, 1024), BF16),
        in_specs=[whole, whole, whole, pl.BlockSpec(memory_space=pltpu.SMEM)],
        out_specs=pl.BlockSpec(memory_space=pltpu.VMEM),
        scratch_shapes=[
            pltpu.VMEM((64, 1024), BF16),
            pltpu.VMEM((16, 1024), BF16),
            pltpu.VMEM((RB, NNZB, BS, BS), BF16),
            pltpu.VMEM((nvec, 8, 128), BF16),
            pltpu.VMEM((nvec, 8, 128), BF16),
            pltpu.VMEM((RB + 2 * HB, 16, BS), BF16),
            pltpu.VMEM((RB + 2 * HB, 16, BS), BF16),
            pltpu.VMEM((RB + 2 * HB, 16, BS), BF16),
            pltpu.VMEM((RB + 2 * HB, 16, BS), BF16),
            pltpu.VMEM((RB, 16, BS), F32),
            pltpu.VMEM((RB, 16, BS), F32),
            pltpu.VMEM((nvec, 8, 128), BF16),
            pltpu.VMEM((nvec, 8, 128), BF16),
            pltpu.VMEM((nrow, nvec, 16, 128), BF16),
            pltpu.VMEM((64, 1024), BF16),
            pltpu.SemaphoreType.DMA((6,)),
            pltpu.SemaphoreType.DMA,
            pltpu.SemaphoreType.DMA,
            pltpu.SemaphoreType.DMA,
            pltpu.SemaphoreType.DMA,
            pltpu.SemaphoreType.DMA((4, 2)),
            pltpu.SemaphoreType.DMA((4, 2)),
            pltpu.SemaphoreType.DMA((5,)),
            pltpu.SemaphoreType.DMA((5,)),
        ],
        compiler_params=pltpu.CompilerParams(
            collective_id=0, has_side_effects=True, vmem_limit_bytes=60 << 20
        ),
    )(vectors[0], rotation.T, blocks, column_blocks.T)
    return out[None]


def solution(mesh):
    placed = (P("row", "vec", None), P(None, "vec"), P("row", None, None, None), P("row", None))
    return jax.shard_map(
        functools.partial(local, mesh.shape["vec"], mesh.shape["row"]),
        mesh=mesh, in_specs=placed, out_specs=P("row", "vec", None), check_vma=False,
    )
```

time: 267 us -> 72 us (0.27)
  waiting for transfers between devices: 168 us -> 0 us
  Pallas kernels: 0 us -> 70.2 us
  matrix products: 28.3 us -> 0 us
  starting transfers between devices: 26.3 us -> 0 us
  blocking collectives: 23.9 us -> 0 us
  between operations: 13.6 us -> 0.01 us
  local copies, waits for them, and re-layouts: 5.21 us -> 1.57 us
    all_gather x1 -> x0, waiting for transfers between devices: 157 us -> none  [local(): lax.all_gather(local_rows, 'vec', axis=0, tiled=True)]
    pallas_call x0 -> x1, Pallas kernels: none -> 70.2 us  [local(): pl.pallas_call(functools.partial(kernel, nvec, nrow), out_shape=jax.Shape...]
    dot_general x5 -> x0, matrix products: 28.3 us -> none  [the longest x4 22.6 us: apply_matrix(): jnp.einsum('rjab,krjb->kra', blocks, picked, preferred_element_type=jnp.f...]
    ppermute x8 -> x0, starting transfers between devices: 26.3 us -> none  [the longest x4 17.3 us: with_halo(): lax.ppermute(lax.slice_in_dim(block, block.shape[dim] - width, None, axis...]
    all_to_all x1 -> x0, blocking collectives: 23.9 us -> none  [local(): lax.all_to_all(filtered, 'vec', split_axis=1, concat_axis=0, tiled=True)]
    ppermute x8 -> x0, waiting for transfers between devices: 10.7 us -> none  [the longest x4 10.7 us: with_halo(): lax.ppermute(lax.slice_in_dim(block, 0, width, axis=dim), axis, backward)]
    gather x4 -> x0, local copies, waits for them, and re-layouts: 3.41 us -> none  [apply_matrix(): picked = stacked[:, offsets]]
  transfers between devices with their start and end apart: 9 -> 0, of which waited for: 5 -> 0; matrix products, arithmetic and copies ran while one was open for 0% -> 0% of each run, Pallas kernels for 0% -> 0%
where the time goes in v1:
time: 72 us; the launch traced here: 71.8 us
  Pallas kernels  70.2 us (98%)
  local copies, waits for them, and re-layouts  1.57 us (2%)
    pallas_call x1, Pallas kernels, local(): pl.pallas_call(functools.partial(kernel, nvec, nrow), out_shape=jax.Shape...  70.2 us
    unnamed x1, local copies, waits for them, and re-layouts  1.57 us

profile of v1, /device:TPU:1, one launch (start us, length us, event | category | flops | bytes accessed | tf_op | source)
XLA Modules:
  0.0 71.8 jit_solution(13418059433155401407)
XLA Ops:
  0.0 70.2 %shard_map.46 = bf16[64,1024]{1,0:T(8,128)(2,1)} custom-call(bf16[64,1024]{1,0:T(8,128)(2,1)} %bitcast.5, bf16[16,1024]{1,0:T(8,128)(2,1)} %bitcast.6, bf16[32,8,128,128]{3,2,1,0:T(8,128)(2,1)} %blk_hbm.1, s32[8,32]{1,0:T(8,128)} %bitcast.7), custom_call_target="tpu_custom_call" | custom-call | tf_op jit(solution)/shard_map/pallas_call | solution.py:262
  70.2 1.6 %copy.6 = bf16[1,64,1024]{2,1,0:T(8,128)(2,1)} copy(bf16[1,64,1024]{2,1,0:T(8,128)(2,1)} %bitcast.4) | data formatting | bytes 262144

commit v2 on v1

--- a/solution.py
+++ b/solution.py
@@ -25,6 +25,10 @@
     pltpu.make_async_copy(ref, ref, sem).wait()
 
 
+def both_ways(q, at, size):
+    return lax.rem(at + (2 * lax.rem(q, 2) - 1) * ((q + 1) // 2) + size, size)
+
+
 def halves(first, second):
     low = lax.broadcasted_iota(jnp.int32, first.shape, first.ndim - 1) < 64
     axis = first.ndim - 1
@@ -36,14 +40,15 @@
 
 def kernel(
     nvec, nrow,
-    v_hbm, rt_hbm, blk_hbm, col, out_ref,
-    v_in, rt_in, blk, send1, recv1, u0, u1, u2, u3, fa, fb, send2, recv2, rall, fbuf,
+    v_hbm, rt_hbm, blk_hbm, col_hbm, out_ref,
+    col, v_in, rt_in, blk, send1, recv1, u0, u1, u2, u3, fa, fb, send2, recv2, rall, fbuf,
     in_sem, s1, r1, s2, r2, hs, hr, gs, gr,
 ):
     me = lax.axis_index("vec")
     row = lax.axis_index("row")
     core = lax.rem(row, CORES)
     yy = me // Z
+    zz = lax.rem(me, Z)
     xs = nrow // CORES
     ys = nvec // Z
     first = row * RB - HB
@@ -54,18 +59,32 @@
         pltpu.make_async_copy(blk_hbm.at[pl.ds(8 * q, 8)], blk.at[pl.ds(8 * q, 8)], in_sem.at[2 + q])
         for q in range(4)
     ]
+    c_copy = pltpu.make_async_copy(col_hbm, col, in_sem.at[6])
     v_copy.start()
     r_copy.start()
+    c_copy.start()
     for c in b_copies:
         c.start()
 
     barrier = pltpu.get_barrier_semaphore()
 
-    def greet(k, _):
-        pl.semaphore_signal(barrier, inc=1, device_id={"vec": lax.rem(me + k, nvec)}, device_id_type=MESH)
-        return 0
-
-    lax.fori_loop(1, nvec, greet, 0)
+    lines = [lax.rem(yy + dy, ys) * Z for dy in (2, 3, 1, 0)]
+
+    def farthest_first(visit):
+        def layer(k, _):
+            z = both_ways(Z - 1 - k, zz, Z)
+            for line in lines:
+                visit(line + z)
+            return 0
+
+        lax.fori_loop(0, Z - 1, layer, 0)
+        for line in lines[:-1]:
+            visit(line + zz)
+
+    def greet(d):
+        pl.semaphore_signal(barrier, inc=1, device_id={"vec": d}, device_id_type=MESH)
+
+    farthest_first(greet)
     for k in range(1, nrow):
         pl.semaphore_signal(barrier, inc=1, device_id={"row": lax.rem(row + k, nrow)}, device_id_type=MESH)
 
@@ -92,17 +111,15 @@
 
     pl.semaphore_wait(barrier, nvec - 1 + nrow - 1)
 
-    def deal(k, _):
-        d = lax.rem(me + k, nvec)
+    def deal(d):
         pltpu.make_async_remote_copy(
             send1.at[d], recv1.at[me], s1, r1, device_id={"vec": d}, device_id_type=MESH
         ).start()
-        return 0
-
-    lax.fori_loop(1, nvec, deal, 0)
+
+    farthest_first(deal)
 
     def along_z(k, _):
-        d = yy * Z + lax.rem(me + k, Z)
+        d = yy * Z + both_ways(Z - k, zz, Z)
         pltpu.make_async_remote_copy(
             rall.at[row, me], rall.at[row, me], gs.at[0], gr.at[0],
             device_id={"vec": d}, device_id_type=MESH,
@@ -137,6 +154,16 @@
         pl.when(row < nrow - 1)(up.wait_send)
         pl.when(row > 0)(down.wait_send)
 
+    for c in b_copies:
+        c.wait()
+
+    def flip(r, _):
+        for j in range(NNZB):
+            blk[r, j] = blk[r, j].T
+        return 0
+
+    lax.fori_loop(0, RB, flip, 0)
+    c_copy.wait()
     take_all(recv1.at[pl.ds(0, nvec - 1)], r1)
     parts = recv1[...].astype(F32).reshape(RB, 2, 8, 128)
     low, high = halves(parts[:, 0], parts[:, 1])
@@ -145,21 +172,10 @@
     fa[...] = start
     halo_start(0, u0)
 
-    take_all(rall.at[0, pl.ds(0, Z - 1)], gr.at[0])
-    for k in range(1, ys):
-        d = lax.rem(me + k * Z, nvec)
-        pltpu.make_async_remote_copy(
-            rall.at[row, pl.ds(yy * Z, Z)], rall.at[row, pl.ds(yy * Z, Z)], gs.at[1], gr.at[1],
-            device_id={"vec": d}, device_id_type=MESH,
-        ).start()
-
-    for c in b_copies:
-        c.wait()
-
     def product(u, r):
         left = jnp.concatenate([u[jnp.clip(col[j, r] - first, 0, RB + 2 * HB - 1)] for j in range(NNZB)], axis=1)
-        right = jnp.concatenate([blk[r, j] for j in range(NNZB)], axis=1)
-        return lax.dot_general(left, right, (((1,), (1,)), ((), ())), preferred_element_type=F32)
+        right = jnp.concatenate([blk[r, j] for j in range(NNZB)], axis=0)
+        return jnp.dot(left, right, preferred_element_type=F32)
 
     def rows_of(turn, u, current, other, following, r):
         if turn == 0:
@@ -181,52 +197,94 @@
             edge(r)
             return 0
 
-        lax.fori_loop(HB, RB - HB, inner, 0, unroll=2)
+        spread(turn)
+        lax.fori_loop(HB, RB - HB, inner, 0, unroll=14)
+
+    mate = row + 1 - 2 * core
+    right = lax.rem(row + CORES, nrow)
+    left = lax.rem(row + nrow - CORES, nrow)
+    opposite = lax.rem(row + 2 * CORES, nrow)
+    half = nvec // 2
+
+    def pass_on(n, held, part, target):
+        piece = rall.at[held, pl.ds(part * half, half)]
+        return pltpu.make_async_remote_copy(
+            piece, piece, gs.at[n], gr.at[n], device_id={"row": target}, device_id_type=MESH
+        )
+
+    def to_mate(n, held):
+        return pltpu.make_async_remote_copy(
+            rall.at[held], rall.at[held], gs.at[n], gr.at[n], device_id={"row": mate}, device_id_type=MESH
+        )
+
+    def spread(turn):
+        if turn == 1:
+            take_all(rall.at[0, pl.ds(0, nvec - Z)], gr.at[1])
+            pass_on(2, row, 0, right).start()
+            pass_on(3, row, 1, left).start()
+            to_mate(8, row).start()
+        if turn == 2:
+            pass_on(4, row, 1, right).start()
+            pass_on(5, row, 0, left).start()
+        if turn == 3:
+            pass_on(2, left, 0, right).wait_recv()
+            pass_on(3, right, 1, left).wait_recv()
+            pass_on(6, left, 0, right).start()
+            pass_on(7, right, 1, left).start()
+
+    take_all(rall.at[0, pl.ds(0, Z - 1)], gr.at[0])
+    for k in range(1, ys):
+        d = lax.rem(me + k * Z, nvec)
+        pltpu.make_async_remote_copy(
+            rall.at[row, pl.ds(yy * Z, Z)], rall.at[row, pl.ds(yy * Z, Z)], gs.at[1], gr.at[1],
+            device_id={"vec": d}, device_id_type=MESH,
+        ).start()
 
     halo_wait(0, u0)
     turn_of(0, u0, fa, fb, u1)
-    take_all(rall.at[0, pl.ds(0, nvec - Z)], gr.at[1])
-    for k in range(1, xs):
-        pltpu.make_async_remote_copy(
-            rall.at[row], rall.at[row], gs.at[2], gr.at[2],
-            device_id={"row": lax.rem(row + k * CORES, nrow)}, device_id_type=MESH,
-        ).start()
-    mate = row + 1 - 2 * core
-    pltpu.make_async_remote_copy(
-        rall.at[row], rall.at[row], gs.at[3], gr.at[3], device_id={"row": mate}, device_id_type=MESH
-    ).start()
     halo_wait(1, u1)
     turn_of(1, u1, fb, fa, u2)
     halo_wait(2, u2)
     turn_of(2, u2, fa, fb, u3)
     halo_wait(3, u3)
-
-    def last(k, _):
-        r = lax.rem(me // 2 + k, RB)
+    zpairs = Z // 2
+
+    def finish(r):
         made = rows_of(3, u3, fb, fa, None, r)
         even, odd = halves(made[:8], made[8:])
         send2[2 * r] = even.astype(BF16)
         send2[2 * r + 1] = odd.astype(BF16)
-        for side in range(2):
-            d = 2 * r + side
-
-            @pl.when(d != me)
-            def _():
-                pltpu.make_async_remote_copy(
-                    send2.at[d], recv2.at[me], s2, r2, device_id={"vec": d}, device_id_type=MESH
-                ).start()
-
+
+    def give(d):
+        @pl.when(d != me)
+        def _():
+            pltpu.make_async_remote_copy(
+                send2.at[d], recv2.at[me], s2, r2, device_id={"vec": d}, device_id_type=MESH
+            ).start()
+
+    def last(g, _):
+        group = [
+            lax.rem(yy + dy, ys) * zpairs + (g + far)
+            for dy in range(ys)
+            for far in (0, zpairs // 2)
+        ]
+        for r in group:
+            finish(r)
+        for r in group:
+            give(2 * r)
+            give(2 * r + 1)
         return 0
 
-    lax.fori_loop(0, RB, last, 0)
+    lax.fori_loop(0, zpairs // 2, last, 0)
     recv2[me] = send2[me]
-
-    take_all(rall.at[pl.ds(0, xs - 1)], gr.at[2])
-    for k in range(1, xs):
-        other = lax.rem(row + k * CORES, nrow)
-        pltpu.make_async_remote_copy(
-            rall.at[other], rall.at[other], gs.at[4], gr.at[4], device_id={"row": mate}, device_id_type=MESH
-        ).start()
+    spread(3)
+    pass_on(4, left, 1, right).wait_recv()
+    pass_on(5, right, 0, left).wait_recv()
+    to_mate(9, left).start()
+    to_mate(10, right).start()
+    pass_on(6, opposite, 0, right).wait_recv()
+    pass_on(7, opposite, 1, left).wait_recv()
+    to_mate(11, opposite).start()
 
     take_all(recv2.at[pl.ds(0, nvec - 1)], r2)
     for t in range(4):
@@ -234,8 +292,8 @@
         fbuf[:, 256 * t : 256 * t + 128] = turned[:64]
         fbuf[:, 256 * t + 128 : 256 * t + 256] = turned[64:]
 
-    take_all(rall.at[0], gr.at[3])
-    take_all(rall.at[pl.ds(0, xs - 1)], gr.at[4])
+    for n in range(8, 12):
+        take_all(rall.at[0], gr.at[n])
     total = jnp.zeros((64, 1024), F32)
     for t in range(4):
         right = jnp.concatenate(
@@ -252,9 +310,10 @@
         halo_sent(step, u)
     take_all(rall.at[0, pl.ds(0, Z - 1)], gs.at[0])
     take_all(rall.at[0, pl.ds(0, nvec - Z)], gs.at[1])
-    take_all(rall.at[pl.ds(0, xs - 1)], gs.at[2])
-    take_all(rall.at[0], gs.at[3])
-    take_all(rall.at[pl.ds(0, xs - 1)], gs.at[4])
+    for n in range(2, 8):
+        take_all(rall.at[0, pl.ds(0, half)], gs.at[n])
+    for n in range(8, 12):
+        take_all(rall.at[0], gs.at[n])
 
 
 def local(nvec, nrow, vectors, rotation, blocks, column_blocks):
@@ -262,9 +321,10 @@
     out = pl.pallas_call(
         functools.partial(kernel, nvec, nrow),
         out_shape=jax.ShapeDtypeStruct((64, 1024), BF16),
-        in_specs=[whole, whole, whole, pl.BlockSpec(memory_space=pltpu.SMEM)],
+        in_specs=[whole] * 4,
         out_specs=pl.BlockSpec(memory_space=pltpu.VMEM),
         scratch_shapes=[
+            pltpu.SMEM((NNZB, RB), jnp.int32),
             pltpu.VMEM((64, 1024), BF16),
             pltpu.VMEM((16, 1024), BF16),
             pltpu.VMEM((RB, NNZB, BS, BS), BF16),
@@ -280,15 +340,15 @@
             pltpu.VMEM((nvec, 8, 128), BF16),
             pltpu.VMEM((nrow, nvec, 16, 128), BF16),
             pltpu.VMEM((64, 1024), BF16),
-            pltpu.SemaphoreType.DMA((6,)),
+            pltpu.SemaphoreType.DMA((7,)),
             pltpu.SemaphoreType.DMA,
             pltpu.SemaphoreType.DMA,
             pltpu.SemaphoreType.DMA,
             pltpu.SemaphoreType.DMA,
             pltpu.SemaphoreType.DMA((4, 2)),
             pltpu.SemaphoreType.DMA((4, 2)),
-            pltpu.SemaphoreType.DMA((5,)),
-            pltpu.SemaphoreType.DMA((5,)),
+            pltpu.SemaphoreType.DMA((12,)),
+            pltpu.SemaphoreType.DMA((12,)),
         ],
         compiler_params=pltpu.CompilerParams(
             collective_id=0, has_side_effects=True, vmem_limit_bytes=60 << 20

time: 72 us -> 53.2 us (0.74)
  Pallas kernels: 70.2 us -> 51.5 us
    pallas_call x1, Pallas kernels: 70.2 us -> 51.5 us  [local(): pl.pallas_call(functools.partial(kernel, nvec, nrow), out_shape=jax.Shape...]
where the time goes in v2:
time: 53.2 us; the launch traced here: 53.1 us
  Pallas kernels  51.5 us (97%)
  local copies, waits for them, and re-layouts  1.57 us (3%)
    pallas_call x1, Pallas kernels, local(): pl.pallas_call(functools.partial(kernel, nvec, nrow), out_shape=jax.Shape...  51.5 us
    unnamed x1, local copies, waits for them, and re-layouts  1.57 us

profile of v2, /device:TPU:1, one launch (start us, length us, event | category | flops | bytes accessed | tf_op | source)
XLA Modules:
  0.0 53.1 jit_solution(4138119276482229635)
XLA Ops:
  0.0 51.5 %shard_map.46 = bf16[64,1024]{1,0:T(8,128)(2,1)} custom-call(bf16[64,1024]{1,0:T(8,128)(2,1)} %bitcast.5, bf16[16,1024]{1,0:T(8,128)(2,1)} %bitcast.6, bf16[32,8,128,128]{3,2,1,0:T(8,128)(2,1)} %blk_hbm.1, s32[8,32]{1,0:T(8,128)} %bitcast.7), custom_call_target="tpu_custom_call" | custom-call | tf_op jit(solution)/shard_map/pallas_call | solution.py:321
  51.5 1.6 %copy.6 = bf16[1,64,1024]{2,1,0:T(8,128)(2,1)} copy(bf16[1,64,1024]{2,1,0:T(8,128)(2,1)} %bitcast.4) | data formatting | bytes 262144

commit v3 on v2

--- a/solution.py
+++ b/solution.py
@@ -351,9 +351,9 @@
             pltpu.SemaphoreType.DMA((12,)),
         ],
         compiler_params=pltpu.CompilerParams(
-            collective_id=0, has_side_effects=True, vmem_limit_bytes=60 << 20
+            collective_id=0, has_side_effects=True, vmem_limit_bytes=50 << 20
         ),
-    )(vectors[0], rotation.T, blocks, column_blocks.T)
+    )(*[pltpu.with_memory_space_constraint(a, pltpu.HBM) for a in (vectors[0], rotation.T, blocks, column_blocks.T)])
     return out[None]
 
 

time: 53.2 us -> 51.6 us (0.970)
  local copies, waits for them, and re-layouts: 1.57 us -> 0.66 us
  Pallas kernels: 51.5 us -> 50.9 us
    unnamed x1, local copies, waits for them, and re-layouts: 1.57 us -> 0.66 us
    pallas_call x1, Pallas kernels: 51.5 us -> 50.9 us  [local(): pl.pallas_call(functools.partial(kernel, nvec, nrow), out_shape=jax.Shape...]
where the time goes in v3:
time: 51.6 us; the launch traced here: 51.5 us
  Pallas kernels  50.9 us (99%)
  local copies, waits for them, and re-layouts  0.66 us (1%)
    pallas_call x1, Pallas kernels, local(): pl.pallas_call(functools.partial(kernel, nvec, nrow), out_shape=jax.Shape...  50.9 us

profile of v3, /device:TPU:1, one launch (start us, length us, event | category | flops | bytes accessed | tf_op | source)
XLA Modules:
  0.0 51.5 jit_solution(12467969464216972750)
XLA Ops:
  0.0 50.9 %shard_map.46 = bf16[64,1024]{1,0:T(8,128)(2,1)S(1)} custom-call(bf16[64,1024]{1,0:T(8,128)(2,1)} %bitcast.5, bf16[16,1024]{1,0:T(8,128)(2,1)} %bitcast.6, bf16[32,8,128,128]{3,2,1,0:T(8,128)(2,1)} %blk_hbm.1, s32[8,32]{1,0:T(8,128)} %bitcast.7), custom_call_target="tpu_custom_call" | custom-call | tf_op jit(solution)/shard_map/pallas_call | solution.py:321
  50.9 0.7 %copy.6 = bf16[1,64,1024]{2,1,0:T(8,128)(2,1)} copy(bf16[1,64,1024]{2,1,0:T(8,128)(2,1)S(1)} %bitcast.4) | data formatting | bytes 262144

commit v4 on v3

--- a/solution.py
+++ b/solution.py
@@ -165,12 +165,16 @@
     lax.fori_loop(0, RB, flip, 0)
     c_copy.wait()
     take_all(recv1.at[pl.ds(0, nvec - 1)], r1)
-    parts = recv1[...].astype(F32).reshape(RB, 2, 8, 128)
-    low, high = halves(parts[:, 0], parts[:, 1])
-    start = jnp.concatenate([low, high], axis=1)
-    u0[pl.ds(HB, RB)] = start.astype(BF16)
-    fa[...] = start
+    def unpack(lo, count):
+        parts = recv1[pl.ds(2 * lo, 2 * count)].astype(F32).reshape(count, 2, 8, 128)
+        rows = jnp.concatenate(halves(parts[:, 0], parts[:, 1]), axis=1)
+        u0[pl.ds(HB + lo, count)] = rows.astype(BF16)
+        fa[pl.ds(lo, count)] = rows
+
+    unpack(0, HB)
+    unpack(RB - HB, HB)
     halo_start(0, u0)
+    unpack(HB, RB - 2 * HB)
 
     def product(u, r):
         left = jnp.concatenate([u[jnp.clip(col[j, r] - first, 0, RB + 2 * HB - 1)] for j in range(NNZB)], axis=1)
@@ -218,35 +222,39 @@
         )
 
     def spread(turn):
-        if turn == 1:
-            take_all(rall.at[0, pl.ds(0, nvec - Z)], gr.at[1])
+        if turn == 2:
             pass_on(2, row, 0, right).start()
             pass_on(3, row, 1, left).start()
-            to_mate(8, row).start()
-        if turn == 2:
+        if turn == 3:
             pass_on(4, row, 1, right).start()
             pass_on(5, row, 0, left).start()
-        if turn == 3:
+        if turn == 4:
             pass_on(2, left, 0, right).wait_recv()
             pass_on(3, right, 1, left).wait_recv()
             pass_on(6, left, 0, right).start()
             pass_on(7, right, 1, left).start()
 
-    take_all(rall.at[0, pl.ds(0, Z - 1)], gr.at[0])
-    for k in range(1, ys):
-        d = lax.rem(me + k * Z, nvec)
-        pltpu.make_async_remote_copy(
-            rall.at[row, pl.ds(yy * Z, Z)], rall.at[row, pl.ds(yy * Z, Z)], gs.at[1], gr.at[1],
-            device_id={"vec": d}, device_id_type=MESH,
-        ).start()
-
+    def along_y():
+        take_all(rall.at[0, pl.ds(0, Z - 1)], gr.at[0])
+        for k in range(1, ys):
+            d = lax.rem(me + k * Z, nvec)
+            pltpu.make_async_remote_copy(
+                rall.at[row, pl.ds(yy * Z, Z)], rall.at[row, pl.ds(yy * Z, Z)], gs.at[1], gr.at[1],
+                device_id={"vec": d}, device_id_type=MESH,
+            ).start()
+
+    pl.when(core == 1)(along_y)
     halo_wait(0, u0)
     turn_of(0, u0, fa, fb, u1)
+    pl.when(core == 0)(along_y)
     halo_wait(1, u1)
     turn_of(1, u1, fb, fa, u2)
+    take_all(rall.at[0, pl.ds(0, nvec - Z)], gr.at[1])
+    to_mate(8, row).start()
     halo_wait(2, u2)
     turn_of(2, u2, fa, fb, u3)
     halo_wait(3, u3)
+    spread(3)
     zpairs = Z // 2
 
     def finish(r):
@@ -277,7 +285,7 @@
 
     lax.fori_loop(0, zpairs // 2, last, 0)
     recv2[me] = send2[me]
-    spread(3)
+    spread(4)
     pass_on(4, left, 1, right).wait_recv()
     pass_on(5, right, 0, left).wait_recv()
     to_mate(9, left).start()

time: 51.6 us -> 49.9 us (0.967)
  Pallas kernels: 50.9 us -> 49.1 us
    pallas_call x1, Pallas kernels: 50.9 us -> 49.1 us  [local(): pl.pallas_call(functools.partial(kernel, nvec, nrow), out_shape=jax.Shape...]
where the time goes in v4:
time: 49.9 us; the launch traced here: 49.8 us
  Pallas kernels  49.1 us (98%)
  local copies, waits for them, and re-layouts  0.66 us (1%)
    pallas_call x1, Pallas kernels, local(): pl.pallas_call(functools.partial(kernel, nvec, nrow), out_shape=jax.Shape...  49.1 us

profile of v4, /device:TPU:1, one launch (start us, length us, event | category | flops | bytes accessed | tf_op | source)
XLA Modules:
  0.0 49.8 jit_solution(10599071529009089021)
XLA Ops:
  0.0 49.1 %shard_map.46 = bf16[64,1024]{1,0:T(8,128)(2,1)S(1)} custom-call(bf16[64,1024]{1,0:T(8,128)(2,1)} %bitcast.5, bf16[16,1024]{1,0:T(8,128)(2,1)} %bitcast.6, bf16[32,8,128,128]{3,2,1,0:T(8,128)(2,1)} %blk_hbm.1, s32[8,32]{1,0:T(8,128)} %bitcast.7), custom_call_target="tpu_custom_call" | custom-call | tf_op jit(solution)/shard_map/pallas_call | solution.py:329
  49.1 0.7 %copy.6 = bf16[1,64,1024]{2,1,0:T(8,128)(2,1)} copy(bf16[1,64,1024]{2,1,0:T(8,128)(2,1)S(1)} %bitcast.4) | data formatting | bytes 262144

commit v5 on v4

--- a/solution.py
+++ b/solution.py
@@ -61,10 +61,6 @@
     ]
     c_copy = pltpu.make_async_copy(col_hbm, col, in_sem.at[6])
     v_copy.start()
-    r_copy.start()
-    c_copy.start()
-    for c in b_copies:
-        c.start()
 
     barrier = pltpu.get_barrier_semaphore()
 
@@ -88,6 +84,10 @@
     for k in range(1, nrow):
         pl.semaphore_signal(barrier, inc=1, device_id={"row": lax.rem(row + k, nrow)}, device_id_type=MESH)
 
+    r_copy.start()
+    c_copy.start()
+    for c in b_copies:
+        c.start()
     v_copy.wait()
     r_copy.wait()
     for t in range(4):
@@ -139,10 +139,15 @@
         )
         return up, down
 
+    def up_start(step, u):
+        pl.when(row < nrow - 1)(halo(step, u)[0].start)
+
+    def down_start(step, u):
+        pl.when(row > 0)(halo(step, u)[1].start)
+
     def halo_start(step, u):
-        up, down = halo(step, u)
-        pl.when(row < nrow - 1)(up.start)
-        pl.when(row > 0)(down.start)
+        up_start(step, u)
+        down_start(step, u)
 
     def halo_wait(step, u):
         up, down = halo(step, u)
@@ -270,20 +275,22 @@
                 send2.at[d], recv2.at[me], s2, r2, device_id={"vec": d}, device_id_type=MESH
             ).start()
 
-    def last(g, _):
-        group = [
-            lax.rem(yy + dy, ys) * zpairs + (g + far)
-            for dy in range(ys)
-            for far in (0, zpairs // 2)
-        ]
-        for r in group:
+    def block_rows(rows):
+        for r in rows:
             finish(r)
-        for r in group:
+        for r in rows:
             give(2 * r)
             give(2 * r + 1)
+
+    def last(g, _):
+        block_rows(
+            [lax.rem(yy + dy, ys) * zpairs + (g + far) for dy in range(ys) for far in (0, zpairs // 2)]
+        )
         return 0
 
-    lax.fori_loop(0, zpairs // 2, last, 0)
+    block_rows([dy * zpairs for dy in range(ys)])
+    block_rows([dy * zpairs + zpairs // 2 for dy in range(ys)])
+    lax.fori_loop(1, zpairs // 2, last, 0)
     recv2[me] = send2[me]
     spread(4)
     pass_on(4, left, 1, right).wait_recv()
@@ -300,16 +307,22 @@
         fbuf[:, 256 * t : 256 * t + 128] = turned[:64]
         fbuf[:, 256 * t + 128 : 256 * t + 256] = turned[64:]
 
-    for n in range(8, 12):
+    for n in range(8, 11):
         take_all(rall.at[0], gr.at[n])
-    total = jnp.zeros((64, 1024), F32)
-    for t in range(4):
-        right = jnp.concatenate(
-            [rall[2 * t].reshape(1024, 128), rall[2 * t + 1].reshape(1024, 128)], axis=1
-        )
-        total += lax.dot_general(
-            fbuf[:, 256 * t : 256 * t + 256], right, (((1,), (1,)), ((), ())), preferred_element_type=F32
-        )
+
+    def turned_by(x):
+        pair = jnp.concatenate(
+            [rall[2 * x].reshape(1024, 128), rall[2 * x + 1].reshape(1024, 128)], axis=1
+        )
+        return lax.dot_general(
+            fbuf[:, pl.ds(pl.multiple_of(256 * x, 256), 256)], pair, (((1,), (1,)), ((), ())),
+            preferred_element_type=F32,
+        )
+
+    chip = row // CORES
+    total = turned_by(chip) + turned_by(lax.rem(chip + 1, xs)) + turned_by(lax.rem(chip + xs - 1, xs))
+    take_all(rall.at[0], gr.at[11])
+    total += turned_by(lax.rem(chip + 2, xs))
     out_ref[...] = total.astype(BF16)
 
     take_all(send1.at[pl.ds(0, nvec - 1)], s1)

time: 49.9 us -> 49.4 us (0.990)
  Pallas kernels: 49.1 us -> 48.6 us
where the time goes in v5:
time: 49.4 us; the launch traced here: 49.3 us
  Pallas kernels  48.6 us (98%)
  local copies, waits for them, and re-layouts  0.66 us (1%)
    pallas_call x1, Pallas kernels, local(): pl.pallas_call(functools.partial(kernel, nvec, nrow), out_shape=jax.Shape...  48.6 us

profile of v5, /device:TPU:1, one launch (start us, length us, event | category | flops | bytes accessed | tf_op | source)
XLA Modules:
  0.0 49.3 jit_solution(10292803997342515329)
XLA Ops:
  0.0 48.6 %shard_map.46 = bf16[64,1024]{1,0:T(8,128)(2,1)S(1)} custom-call(bf16[64,1024]{1,0:T(8,128)(2,1)} %bitcast.5, bf16[16,1024]{1,0:T(8,128)(2,1)} %bitcast.6, bf16[32,8,128,128]{3,2,1,0:T(8,128)(2,1)} %blk_hbm.1, s32[8,32]{1,0:T(8,128)} %bitcast.7), custom_call_target="tpu_custom_call" | custom-call | tf_op jit(solution)/shard_map/pallas_call | solution.py:342
  48.6 0.7 %copy.6 = bf16[1,64,1024]{2,1,0:T(8,128)(2,1)} copy(bf16[1,64,1024]{2,1,0:T(8,128)(2,1)S(1)} %bitcast.4) | data formatting | bytes 262144

commit v6 on v5

--- a/solution.py
+++ b/solution.py
@@ -198,9 +198,17 @@
 
     def turn_of(turn, u, current, other, following):
         edge = functools.partial(rows_of, turn, u, current, other, following)
-        for r in (0, 1, RB - 2, RB - 1):
-            edge(r)
-        halo_start(turn + 1, following)
+        for side in (core, 1 - core):
+            for r in range(HB):
+                edge((RB - HB) * side + r)
+
+            @pl.when(side == 1)
+            def _():
+                up_start(turn + 1, following)
+
+            @pl.when(side == 0)
+            def _():
+                down_start(turn + 1, following)
 
         def inner(r, _):
             edge(r)

time: 49.4 us -> 49.2 us (level)
  no operation moved by 1% of the time
where the time goes in v6:
time: 49.2 us; the launch traced here: 49 us
  Pallas kernels  48.4 us (98%)
  local copies, waits for them, and re-layouts  0.66 us (1%)
    pallas_call x1, Pallas kernels, local(): pl.pallas_call(functools.partial(kernel, nvec, nrow), out_shape=jax.Shape...  48.4 us

profile of v6, /device:TPU:1, one launch (start us, length us, event | category | flops | bytes accessed | tf_op | source)
XLA Modules:
  0.0 49.0 jit_solution(17169583821234084483)
XLA Ops:
  0.0 48.4 %shard_map.46 = bf16[64,1024]{1,0:T(8,128)(2,1)S(1)} custom-call(bf16[64,1024]{1,0:T(8,128)(2,1)} %bitcast.5, bf16[16,1024]{1,0:T(8,128)(2,1)} %bitcast.6, bf16[32,8,128,128]{3,2,1,0:T(8,128)(2,1)} %blk_hbm.1, s32[8,32]{1,0:T(8,128)} %bitcast.7), custom_call_target="tpu_custom_call" | custom-call | tf_op jit(solution)/shard_map/pallas_call | solution.py:350
  48.4 0.7 %copy.6 = bf16[1,64,1024]{2,1,0:T(8,128)(2,1)} copy(bf16[1,64,1024]{2,1,0:T(8,128)(2,1)S(1)} %bitcast.4) | data formatting | bytes 262144
